TPU v7x, 32 devices: a whole 2x2x4 slice. The times are simulated.
32 devices in a mesh: frow: 4 (over z), fcol: 4 (over x, core), chan: 2 (over y).
Axes of the slice: x: 2, y: 2, z: 4, core: 2. Of those that a mesh axis runs over, the one named last changes fastest.
Arguments:
- image_cube: float32 [32, 256, 1024], P('chan', 'frow', 'fcol'), may hold values from -40 to 40
- weights: float32 [3, 256, 1024], P(None, 'frow', 'fcol'), may hold values from 0.5 to 2
Outputs:
- backprojected: float32 [32, 256, 1024], P('chan', 'frow', 'fcol')
- lowrank: float32 [32, 256, 1024], P('chan', 'frow', 'fcol')
All inputs are finite; a program needn't handle non-finite values.
Results may differ from a plain program's by a relative error of at most 0.0003.
Values sent between devices are 32-bit elements; how exact they have to be, the bound alone decides.
A program may use at most 128 MiB of HBM per device.

v0:
```python
import functools
import math

import jax
import jax.numpy as jnp
from jax import lax
from jax.experimental import pallas as pl
from jax.experimental.pallas import tpu as pltpu
from jax.sharding import PartitionSpec as P

JSWEEPS = 3


filter_taps = (0.0625, 0.25, 0.375, 0.25, 0.0625)
band_levels = (12.0, 4.0, 2.5)
rank_level = 2.0
tiny_value = 1e-30


def rank_round(state, marks):
    quads, sides, labels, cosine, sine = state
    eye, lane, row, first_mask, last_mask, step_mask, last = marks
    upper_left, upper_right, lower_left, lower_right = quads
    side_top, side_bottom = sides
    label_top, label_bottom = labels

    def across(values):
        return jnp.sum(jnp.where(eye, values, 0.0), axis=0, keepdims=True)

    cosine_row = across(cosine)
    sine_row = across(sine)

    def turn_rows(top, bottom):
        return cosine * top - sine * bottom, sine * top + cosine * bottom

    def move_rows(top, bottom):
        up = pltpu.roll(jnp.where(row == 0, bottom, top), 1, 0)
        down = pltpu.roll(bottom, last, 0)
        return jnp.where(row == 0, top, up), jnp.where(row == last, top, down)

    def turn_cols(left, right):
        return cosine_row * left - sine_row * right, sine_row * left + cosine_row * right

    def move_cols(left, right):
        ahead = pltpu.roll(jnp.where(lane == 0, right, left), 1, 1)
        back = pltpu.roll(right, lane.shape[1] - 1, 1)
        return jnp.where(lane == 0, left, ahead), jnp.where(lane == last, left, back)

    upper_left, lower_left = move_rows(*turn_rows(upper_left, lower_left))
    upper_right, lower_right = move_rows(*turn_rows(upper_right, lower_right))
    upper_left, upper_right = turn_cols(upper_left, upper_right)
    lower_left, lower_right = turn_cols(lower_left, lower_right)
    sides = move_rows(*turn_rows(side_top, side_bottom))
    label_top, label_bottom = move_rows(label_top, label_bottom)
    own_top = jnp.where(step_mask, upper_left, jnp.where(first_mask, upper_right, 0.0))
    next_mask = lane == row + 1
    own_bottom = jnp.where(
        next_mask & (row < last), lower_right, jnp.where(last_mask, lower_left, 0.0)
    )
    pair = jnp.where(next_mask & (row < last), upper_right, jnp.where(last_mask, upper_left, 0.0))
    gap = jnp.sum(own_bottom - own_top, axis=1, keepdims=True)
    cross = jnp.sum(pair, axis=1, keepdims=True)
    cosine, sine = turn_of(gap, cross, label_top < label_bottom)
    upper = move_cols(upper_left, upper_right)
    lower = move_cols(lower_left, lower_right)
    return (upper + lower, sides, (label_top, label_bottom), cosine, sine)


def turn_of(gap, cross, ordered):
    gap = jnp.broadcast_to(gap, ordered.shape)
    cross = jnp.broadcast_to(cross, ordered.shape)
    positive = (gap > 0) | ((gap == 0) & ordered)
    double = 2.0 * cross
    root = jnp.sqrt(gap * gap + double * double)
    tangent = jnp.where(positive, double, -double) / (jnp.abs(gap) + root + tiny_value)
    cosine = lax.rsqrt(1.0 + tangent * tangent)
    return cosine, tangent * cosine


def rank_start(gram):
    order = gram.shape[0]
    half, last, lanes = order // 2, order // 2 - 1, 128
    highest = lax.Precision.HIGHEST
    row = lax.broadcasted_iota(jnp.int32, (half, lanes), 0)
    lane = lax.broadcasted_iota(jnp.int32, (half, lanes), 1)
    eye = lane == row
    first_mask = (row == 1) & (lane == 0)
    last_mask = (row == last) & (lane == last)
    step_mask = ((row == 0) & (lane == 0)) | ((row >= 2) & (lane == row - 1))
    marks = (eye, lane, row, first_mask, last_mask, step_mask, last)
    mirror = lane == order - 1 - row
    pick_row = lax.broadcasted_iota(jnp.int32, (order, lanes), 0)
    pick_lane = lax.broadcasted_iota(jnp.int32, (order, lanes), 1)
    one = lambda mask: jnp.where(mask, 1.0, 0.0)
    pick_left = one((pick_row == pick_lane) & (pick_lane < half))
    pick_right = one((pick_row == order - 1 - pick_lane) & (pick_lane < half))
    dot = functools.partial(jnp.dot, precision=highest, preferred_element_type=jnp.float32)
    flip_row = lax.broadcasted_iota(jnp.int32, (half, half), 0)
    flip_lane = lax.broadcasted_iota(jnp.int32, (half, half), 1)
    flip = one(flip_row + flip_lane == last)
    top, bottom = gram[:half], dot(flip, gram[half:])
    quads = (dot(top, pick_left), dot(top, pick_right), dot(bottom, pick_left), dot(bottom, pick_right))
    sides = (one(eye), one(mirror))
    labels = (row, order - 1 - row)
    total = lambda values: jnp.sum(jnp.where(eye, values, 0.0), axis=1, keepdims=True)
    cosine, sine = turn_of(
        total(quads[3] - quads[0]), total(quads[1]), labels[0] < labels[1]
    )
    return (quads, sides, labels, cosine, sine), marks


def rank_finish(state, marks, threshold):
    highest = lax.Precision.HIGHEST
    eye = marks[0]
    total = lambda values: jnp.sum(jnp.where(eye, values, 0.0), axis=1, keepdims=True)
    quads, sides = state[0], state[1]
    mixing = 0.0
    for quad, side in zip((quads[0], quads[3]), sides):
        values = total(quad)
        factor = 1.0 - threshold / jnp.sqrt(jnp.maximum(values, threshold * threshold))
        mixing = mixing + lax.dot_general(
            side * factor, side, (((0,), (0,)), ((), ())), precision=highest,
            preferred_element_type=jnp.float32,
        )
    order = 2 * eye.shape[0]
    return mixing[:order, :order]


def spread(x, dilation):
    for axis in (0, 1):
        size = x.shape[axis]
        pair = x + pltpu.roll(x, 2 * dilation, axis)
        ends = pair + pltpu.roll(pair, size - 2 * dilation, axis)
        x = ends + 4.0 * (x + pltpu.roll(pair, size - dilation, axis))
    return x * (filter_taps[0] * filter_taps[0])


def split_two(values):
    high = values.astype(jnp.bfloat16)
    low = (values - high.astype(jnp.float32)).astype(jnp.bfloat16)
    return high, low


def facet_kernel(
    threshold, image_ref, weights_ref, back_ref, rank_ref,
    wide, bands, sums, other_sums, diffs, full, gram, other_gram, mixing,
    pack_out, pack_in, pack_out_two, pack_in_two, send_sems, recv_sems, local_sems,
):
    channels, rows, cols = image_ref.shape
    pixels = rows * cols
    part = pixels // 2
    names = ("frow", "fcol", "chan")
    place = {name: lax.axis_index(name) for name in names}
    count = {name: lax.axis_size(name) for name in names}
    me = place["chan"]
    partner = 1 - me
    has = {
        ("frow", 1): place["frow"] < count["frow"] - 1,
        ("frow", -1): place["frow"] > 0,
        ("fcol", 1): place["fcol"] < count["fcol"] - 1,
        ("fcol", -1): place["fcol"] > 0,
    }
    barrier = pltpu.get_barrier_semaphore()
    mesh_ids = pl.DeviceIdType.MESH

    def target(name, step):
        ids = dict(place)
        ids[name] = place[name] + step
        return tuple(ids[key] for key in names)

    def mate():
        return (place["frow"], place["fcol"], partner)

    def copy_to(index, source, sink, device):
        return pltpu.make_async_remote_copy(
            src_ref=source, dst_ref=sink, send_sem=send_sems.at[index],
            recv_sem=recv_sems.at[index], device_id=device, device_id_type=mesh_ids,
        )

    own_rows = pl.ds(pl.multiple_of(me * channels, channels), channels)
    to_mate = pl.ds(pl.multiple_of(partner * part, part), part)
    to_self = pl.ds(pl.multiple_of(me * part, part), part)
    keep_image = pltpu.make_async_copy(
        image_ref, wide.at[:, pl.ds(8, rows), :], local_sems.at[0]
    )
    keep_image.start()

    zero_rows = jnp.zeros((channels, 8, cols), jnp.float32)

    @pl.when(jnp.logical_not(has["frow", -1]))
    def _():
        wide[:, 0:8, :] = zero_rows
        diffs[0, :, 0:8, :] = zero_rows
        diffs[1, :, 0:8, :] = zero_rows

    @pl.when(jnp.logical_not(has["frow", 1]))
    def _():
        wide[:, rows + 8 : rows + 16, :] = zero_rows
        diffs[0, :, rows + 8 : rows + 16, :] = zero_rows
        diffs[1, :, rows + 8 : rows + 16, :] = zero_rows

    for side, step in ((0, -1), (1, 1)):

        @pl.when(jnp.logical_not(has["fcol", step]))
        def _(side=side):
            pack_in[side] = jnp.zeros(pack_in.shape[1:], jnp.float32)
            pack_in_two[side] = jnp.zeros(pack_in_two.shape[1:], jnp.float32)

    pl.semaphore_signal(barrier, inc=1, device_id=mate(), device_id_type=mesh_ids)
    friends = 1
    for key in has:

        @pl.when(has[key])
        def _(key=key):
            pl.semaphore_signal(barrier, inc=1, device_id=target(*key), device_id_type=mesh_ids)

        friends = friends + jnp.where(has[key], 1, 0)
    pl.semaphore_wait(barrier, friends)

    first_part = copy_to(0, full.at[own_rows, to_mate], full.at[own_rows, to_mate], mate())
    second_part = copy_to(1, full.at[own_rows, to_self], full.at[own_rows, to_self], mate())
    below = lambda ref, at: ref.at[..., pl.ds(at, 8), :]

    def row_copies(index, source, offset, sink):
        return (
            (("frow", 1), ("frow", -1), copy_to(
                index, below(source, offset + rows - 8), below(sink, 0), target("frow", 1))),
            (("frow", -1), ("frow", 1), copy_to(
                index + 1, below(source, offset), below(sink, rows + 8), target("frow", -1))),
        )

    def col_copies(index, source, sink):
        return (
            (("fcol", 1), ("fcol", -1), copy_to(
                index, source.at[1], sink.at[0], target("fcol", 1))),
            (("fcol", -1), ("fcol", 1), copy_to(
                index + 1, source.at[0], sink.at[1], target("fcol", -1))),
        )

    def start_all(copies):
        for goes, _, copy in copies:

            @pl.when(has[goes])
            def _(copy=copy):
                copy.start()

    def arrive_all(copies):
        for _, comes, copy in copies:

            @pl.when(has[comes])
            def _(copy=copy):
                copy.wait_recv()

    def left_all(copies):
        for goes, _, copy in copies:

            @pl.when(has[goes])
            def _(copy=copy):
                copy.wait_send()

    rows_one = row_copies(2, image_ref, 0, wide)
    cols_one = col_copies(4, pack_out, pack_in)
    rows_two = row_copies(8, diffs, 8, diffs)
    cols_two = col_copies(10, pack_out_two, pack_in_two)
    start_all(rows_one)
    keep_image.wait()

    def flatten(at):
        group = jnp.swapaxes(wide[:, pl.ds(pl.multiple_of(at + 8, 8), 8), :], 0, 1)
        for row in range(8):
            where = pl.multiple_of((at + row) * cols, cols)
            full[own_rows, pl.ds(where, cols)] = group[row]

    def flatten_part(which):
        def body(step, carried):
            flatten(pl.multiple_of(which * (rows // 2) + step * 8, 8))
            return carried

        lax.fori_loop(0, rows // 16, body, 0)

    flatten_part(partner)
    first_part.start()
    flatten_part(me)

    tall = rows + 16
    tile_lane = lax.broadcasted_iota(jnp.int32, (tall, 128), 1)

    def pack_edges(load, store):
        def body(ch, sides):
            left, right = sides
            here = (tile_lane >= ch * 8) & (tile_lane < ch * 8 + 8)
            tile_first = pltpu.roll(load(ch, pl.ds(0, 128)), ch * 8, 1)
            tile_last = pltpu.roll(load(ch, pl.ds(cols - 128, 128)), ch * 8 + 8, 1)
            return jnp.where(here, tile_first, left), jnp.where(here, tile_last, right)

        empty = jnp.zeros((tall, 128), jnp.float32)
        left, right = lax.fori_loop(0, channels, body, (empty, empty))
        store(0, left)
        store(1, right)

    def edge_tile(ch, before, after):
        after = pltpu.roll(after, 128 - ch * 8, 1)
        before = pltpu.roll(before, 120 - ch * 8, 1)
        return jnp.where(tile_lane < 8, after, jnp.where(tile_lane >= 120, before, 0.0))

    long = cols + 128
    row_at = lax.broadcasted_iota(jnp.int32, (tall, long), 0) - 8
    col_at = lax.broadcasted_iota(jnp.int32, (tall, long), 1)
    col_at = jnp.where(col_at < cols + 64, col_at, col_at - long)
    row_at = row_at + place["frow"] * rows
    col_at = col_at + place["fcol"] * cols
    valid = (row_at >= 0) & (row_at < count["frow"] * rows)
    valid = valid & (col_at >= 0) & (col_at < count["fcol"] * cols)
    inside = lambda values: jnp.where(valid, values, 0.0)

    arrive_all(rows_one)
    pack_edges(lambda ch, at: wide[ch, :, at], pack_out.__setitem__)
    start_all(cols_one)
    sums[...] = jnp.zeros(sums.shape, jnp.float32)
    arrive_all(cols_one)

    def analyse(ch, carried):
        center = wide[ch]
        tile = edge_tile(ch, pack_in[0], pack_in[1])
        coarse_one = inside(spread(jnp.concatenate([center, tile], axis=1), 1))
        coarse_two = spread(coarse_one, 2)[8 : rows + 8, :cols]
        coarse_one = coarse_one[8 : rows + 8, :cols]
        for index, band in enumerate(
            (center[8 : rows + 8] - coarse_one, coarse_one - coarse_two, coarse_two)
        ):
            bands[index, ch] = band
            sums[index] = sums[index] + band * band
        return carried

    lax.fori_loop(0, channels, analyse, 0)
    share_sums = copy_to(6, sums, other_sums, mate())

    first_part.wait_recv()
    order = 2 * channels
    block = 1024
    start = me * part

    def gram_step(step, total):
        at = pl.ds(pl.multiple_of(start + step * block, block), block)
        both = jnp.concatenate(split_two(full[:, at]), axis=0)
        return total + lax.dot_general(
            both, both, (((1,), (1,)), ((), ())), preferred_element_type=jnp.float32
        )

    product = lax.fori_loop(
        0, part // block, gram_step, jnp.zeros((2 * order, 2 * order), jnp.float32)
    )
    gram[:, :order] = (
        product[:order, :order] + (product[:order, order:] + product[order:, :order])
    ) + product[order:, order:]
    share_gram = copy_to(7, gram, other_gram, mate())
    share_gram.start()

    share_sums.start()
    second_part.start()

    share_gram.wait_recv()
    state, marks = rank_start(gram[:, :order] + other_gram[:, :order])
    rounds = JSWEEPS * (order - 1)
    turn = lambda _, carried: rank_round(carried, marks)
    state = lax.fori_loop(0, 3 * rounds // 10, turn, state)
    share_sums.wait_recv()
    for index in range(3):
        levels = band_levels[index] * weights_ref[index]
        totals = sums[index] + other_sums[index]
        other_sums[index] = levels / jnp.sqrt(jnp.maximum(totals, levels * levels))

    def project(ch, carried):
        duals = [bands[index, ch] * other_sums[index] for index in range(3)]
        back_ref[ch] = duals[0]
        diffs[0, ch, pl.ds(8, rows), :] = duals[1] - duals[0]
        diffs[1, ch, pl.ds(8, rows), :] = duals[2] - duals[1]
        return carried

    lax.fori_loop(0, channels, project, 0)
    start_all(rows_two)
    state = lax.fori_loop(3 * rounds // 10, 8 * rounds // 10, turn, state)
    arrive_all(rows_two)
    for index in range(2):
        pack_edges(
            lambda ch, at, index=index: diffs[index, ch, :, at],
            lambda side, value, index=index: pack_out_two.__setitem__((side, index), value),
        )
    start_all(cols_two)
    state = lax.fori_loop(8 * rounds // 10, rounds, turn, state)
    mixing[:, :order] = rank_finish(state, marks, threshold)

    arrive_all(cols_two)

    def synthesise(ch, carried):
        outer, inner = [
            jnp.concatenate(
                [diffs[index, ch], edge_tile(ch, pack_in_two[0, index], pack_in_two[1, index])],
                axis=1,
            )
            for index in range(2)
        ]
        summed = inside(outer + spread(inner, 2))
        back_ref[ch] = back_ref[ch] + spread(summed, 1)[8 : rows + 8, :cols]
        return carried

    lax.fori_loop(0, channels, synthesise, 0)

    second_part.wait_recv()
    high, low = split_two(mixing[own_rows, :order])
    left = jnp.concatenate([high, high, low, low], axis=1)

    def rank_step(step, carried):
        at = pl.ds(pl.multiple_of(step * block, block), block)
        high, low = split_two(full[:, at])
        right = jnp.concatenate([high, low, high, low], axis=0)
        rank_ref[:, at] = jnp.dot(left, right, preferred_element_type=jnp.float32)
        return carried

    lax.fori_loop(0, pixels // block, rank_step, 0)
    for copies in (rows_one, cols_one, rows_two, cols_two):
        left_all(copies)
    for copy in (first_part, second_part, share_sums, share_gram):
        copy.wait_send()


def shards(image_cube, weights):
    channels, rows, cols = image_cube.shape
    pixels = rows * cols
    threshold = rank_level * math.sqrt(pixels)
    order = channels * lax.axis_size("chan")
    tall = rows + 16
    f32 = jnp.float32
    anywhere = pl.BlockSpec(memory_space=pl.ANY)
    in_vmem = pl.BlockSpec(memory_space=pltpu.VMEM)
    back, rank = pl.pallas_call(
        functools.partial(facet_kernel, threshold),
        out_shape=(
            jax.ShapeDtypeStruct(image_cube.shape, f32),
            jax.ShapeDtypeStruct((channels, pixels), f32),
        ),
        in_specs=[anywhere, in_vmem],
        out_specs=(in_vmem, in_vmem),
        scratch_shapes=[
            pltpu.VMEM((channels, tall, cols), f32),
            pltpu.VMEM((3, channels, rows, cols), f32),
            pltpu.VMEM((3, rows, cols), f32),
            pltpu.VMEM((3, rows, cols), f32),
            pltpu.VMEM((2, channels, tall, cols), f32),
            pltpu.VMEM((order, pixels), f32),
            pltpu.VMEM((order, 128), f32),
            pltpu.VMEM((order, 128), f32),
            pltpu.VMEM((order, 128), f32),
            pltpu.VMEM((2, tall, 128), f32),
            pltpu.VMEM((2, tall, 128), f32),
            pltpu.VMEM((2, 2, tall, 128), f32),
            pltpu.VMEM((2, 2, tall, 128), f32),
            pltpu.SemaphoreType.DMA((12,)),
            pltpu.SemaphoreType.DMA((12,)),
            pltpu.SemaphoreType.DMA((1,)),
        ],
        compiler_params=pltpu.CompilerParams(
            collective_id=0, has_side_effects=True, vmem_limit_bytes=50 * 2**20
        ),
    )(image_cube, weights)
    return back, rank.reshape(image_cube.shape)


def solution(mesh):
    placed = (P("chan", "frow", "fcol"), P(None, "frow", "fcol"))
    return jax.shard_map(
        shards,
        mesh=mesh,
        in_specs=placed,
        out_specs=(P("chan", "frow", "fcol"), P("chan", "frow", "fcol")),
        check_vma=False,
    )
```

profile of v0, /device:TPU:1, one launch (start us, length us, event | category | flops | bytes accessed | tf_op | source)
XLA Modules:
  0.0 57.3 jit_solution(12935196090828973606)
XLA Ops:
  0.6 0.0 copy-start
  0.6 1.2 %copy-done = f32[16,64,256]{2,1,0:T(8,128)S(1)} copy-done((f32[16,64,256]{2,1,0:T(8,128)S(1)}, f32[16,64,256]{2,1,0:T(8,128)}, u32[]{:S(2)}) %copy-start) | copy-done | bytes 1048600
  1.9 0.0 copy-start.1
  1.9 0.9 %copy-done.1 = f32[3,64,256]{2,1,0:T(8,128)S(1)} copy-done((f32[3,64,256]{2,1,0:T(8,128)S(1)}, f32[3,64,256]{2,1,0:T(8,128)}, u32[]{:S(2)}) %copy-start.1) | copy-done | bytes 196632
  2.8 52.3 %shard_map.41 = (f32[16,64,256]{2,1,0:T(8,128)S(1)}, f32[16,16384]{1,0:T(8,128)S(1)}) custom-call(f32[16,64,256]{2,1,0:T(8,128)S(1)} %copy-done, f32[3,64,256]{2,1,0:T(8,128)S(1)} %copy-done.1), custom_call_target="tpu_custom_call" | custom-call | tf_op jit(solution)/shard_map/pallas_call | solution.py:436
  55.1 1.3 %copy.4 = f32[2,8,64,256]{3,2,1,0:T(8,128)} copy(f32[2,8,64,256]{3,1,2,0:T(8,128)S(1)} %bitcast.2) | data formatting | bytes 2097152
  56.4 1.0 %copy.6 = f32[16,64,256]{2,1,0:T(8,128)} copy(f32[16,64,256]{2,1,0:T(8,128)S(1)} %get-tuple-element.8) | data formatting | bytes 2097152
Async XLA Ops:
  0.6 1.2 %copy-start = (f32[16,64,256]{2,1,0:T(8,128)S(1)}, f32[16,64,256]{2,1,0:T(8,128)}, u32[]{:S(2)}) copy-start(f32[16,64,256]{2,1,0:T(8,128)} %image_ref.1) | copy-start | bytes 3145732
  1.9 0.9 %copy-start.1 = (f32[3,64,256]{2,1,0:T(8,128)S(1)}, f32[3,64,256]{2,1,0:T(8,128)}, u32[]{:S(2)}) copy-start(f32[3,64,256]{2,1,0:T(8,128)} %weights_ref.1) | copy-start | bytes 589828
where the time goes:
time: 57.5 us; the launch traced here: 57.3 us
  Pallas kernels  52.3 us (91%)
  local copies, waits for them, and re-layouts  4.4 us (8%)
  between operations  0.65 us (1%)
    pallas_call x1, Pallas kernels, shards(): pl.pallas_call(functools.partial(facet_kernel, threshold), out_shape=(jax...  52.3 us
    unnamed x6, local copies, waits for them, and re-layouts  4.4 us

commit v1 on v0

v1 whole, which is shorter than its diff:
```python
import functools
import math

import jax
import jax.numpy as jnp
from jax import lax
from jax.experimental import pallas as pl
from jax.experimental.pallas import tpu as pltpu
from jax.sharding import PartitionSpec as P

JSWEEPS = 3
HALO = 8
REACH = 6
NEAR = 2
PACK = 16
CHUNK = 8
TURNS = 3

filter_taps = (0.0625, 0.25, 0.375, 0.25, 0.0625)
band_levels = (12.0, 4.0, 2.5)
rank_level = 2.0


def down(x, row):
    top, low = x[:8], x[8:]
    a, b = pltpu.roll(top, 1, 0), pltpu.roll(low, 1, 0)
    first = row == 0
    return jnp.concatenate([jnp.where(first, top, a), jnp.where(first, a, b)], axis=0)

def up(x, row):
    top, low = x[:8], x[8:]
    a, b = pltpu.roll(top, 7, 0), pltpu.roll(low, 7, 0)
    final = row == 7
    return jnp.concatenate([jnp.where(final, b, a), jnp.where(final, low, b)], axis=0)

def lanes(x):
    return jnp.broadcast_to(jnp.sum(x, axis=1, keepdims=True), x.shape)

def moved(state, row):
    bt, bl, wt, wl = state
    return [down(v, row) for v in (bt, bl, wt, wl)], [up(v, row) for v in (bt, bl, wt, wl)]

def ahead(moves):
    (bt, bl, _, _), (_, _, wt, wl) = moves
    return lanes(bt * wt), lanes(bt * wl), lanes(bl * wt), lanes(bl * wl)

def rotation(gap, cross, first):
    double = cross + cross
    size = gap * gap + double * double
    flat = size < 1e-36
    inverse = lax.rsqrt(jnp.maximum(size, 1e-36))
    positive = (gap > 0) | ((gap == 0) & first)
    square = jnp.where(flat, 1.0, 0.5 + (0.5 * jnp.abs(gap)) * inverse)
    part = jnp.where(flat, 0.0, jnp.where(positive, cross, -cross) * inverse)
    root = lax.rsqrt(square)
    sine = part * root
    return square * root, sine, sine * root * cross

def rank_round(carry, tie, marks):
    vectors, diag, dots, turn = carry
    row, second, final = marks
    (cosine, sine, shift) = turn
    top, low = diag[0] - shift, diag[1] + shift
    cd, sd, cu, su = down(cosine, row), down(sine, row), up(cosine, row), up(sine, row)
    alpha, beta = jnp.where(second, sd, cd), jnp.where(second, cd, -sd)
    gamma, delta = jnp.where(final, cu, su), jnp.where(final, -su, cu)
    cross = alpha * (gamma * dots[0] + delta * dots[1]) + beta * (gamma * dots[2] + delta * dots[3])
    new_top = jnp.where(second, down(low, row), down(top, row))
    new_low = jnp.where(final, up(top, row), up(low, row))
    turn = rotation(new_low - new_top, cross, tie)
    (dbt, dbl, dwt, dwl), (ubt, ubl, uwt, uwl) = moved(vectors, row)
    vectors = (alpha * dbt + beta * dbl, gamma * ubt + delta * ubl, alpha * dwt + beta * dwl, gamma * uwt + delta * uwl)
    return vectors, (new_top, new_low), ahead(moved(vectors, row)), turn

def first_on_top(index, shape):
    place = lax.broadcasted_iota(jnp.int32, shape, 0)
    cycle = 2 * shape[0] - 1
    top = place - 1 - index
    top = jnp.where(place == 0, -1, jnp.where(top < 0, top + cycle, top))
    low = cycle - 1 - place - index
    low = jnp.where(low < 0, low + cycle, low)
    return top < low


def rank_start(gram, marks):
    row = marks[0]
    half = gram.shape[0] // 2
    shape = (half, gram.shape[1])
    place = lax.broadcasted_iota(jnp.int32, shape, 0)
    lane = lax.broadcasted_iota(jnp.int32, shape, 1)
    flip_row = lax.broadcasted_iota(jnp.int32, (half, half), 0)
    flip_lane = lax.broadcasted_iota(jnp.int32, (half, half), 1)
    flip = jnp.where(flip_row + flip_lane == half - 1, 1.0, 0.0)
    low = jnp.dot(
        flip, gram[half:], precision=lax.Precision.HIGHEST, preferred_element_type=jnp.float32
    )
    sides = (jnp.where(lane == place, 1.0, 0.0), jnp.where(lane == 2 * half - 1 - place, 1.0, 0.0))
    vectors = (gram[:half], low, *sides)
    diag = (lanes(gram[:half] * sides[0]), lanes(low * sides[1]))
    turn = rotation(diag[1] - diag[0], lanes(gram[:half] * sides[1]), first_on_top(0, shape))
    return vectors, diag, ahead(moved(vectors, row)), turn


def rank_finish(carry, threshold):
    vectors, diag = carry[0], carry[1]
    mixing = 0.0
    for side, values in zip(vectors[2:], diag):
        factor = 1.0 - threshold / jnp.sqrt(jnp.maximum(values, threshold * threshold))
        mixing = mixing + lax.dot_general(
            side * factor, side, (((0,), (0,)), ((), ())),
            precision=lax.Precision.HIGHEST, preferred_element_type=jnp.float32,
        )
    return mixing


def split_two(values):
    high = values.astype(jnp.bfloat16)
    low = (values - high.astype(jnp.float32)).astype(jnp.bfloat16)
    return high, low


def tap(offset):
    near = jnp.abs(offset)
    return jnp.where(
        near == 0, filter_taps[2],
        jnp.where(near == 1, filter_taps[3], jnp.where(near == 2, filter_taps[4], 0.0)),
    )


def column_weights(start, total):
    shape = (256, 128)
    source = lax.broadcasted_iota(jnp.int32, shape, 0)
    target = lax.broadcasted_iota(jnp.int32, shape, 1)
    source = jnp.where(source < 192, source, source - 256)
    scale = filter_taps[0]
    one = tap(source - target) * scale
    forward, backward = 0.0, 0.0
    for step in range(-2, 3):
        weight = filter_taps[step + 2] * scale * scale
        between = target + 2 * step
        keep = (between + start >= 0) & (between + start < total)
        forward = forward + jnp.where(keep, weight * tap(source - between), 0.0)
        between = target + step
        keep = (between + start >= 0) & (between + start < total)
        away = source - between
        wide = jnp.where(away % 2 == 0, tap(away // 2), 0.0)
        backward = backward + jnp.where(keep, weight * wide, 0.0)
    return one, forward, backward


def rows_filter(ref, at, count, dilation):
    part = lambda step: ref[pl.ds(at + step * dilation, count)]
    return (part(-2) + part(2)) + 4.0 * (part(-1) + part(1)) + 6.0 * part(0)


def facet_kernel(
    threshold, image_ref, weights_ref, back_ref, rank_ref,
    raw, factors, cube, one_cols, two_cols, middle, coarse, level_rows, sums, other_sums,
    duals, diffs, gram, other_gram, mixing, taps_one, taps_two,
    strips_out, strips_in, corners_in, strips_out_two, strips_in_two, corners_in_two,
    send_sems, recv_sems, local_sems,
):
    channels, rows, cols = image_ref.shape
    wide = cols // 2
    half = rows // 2
    chunks = half // CHUNK
    groups = rows // PACK
    order = 2 * channels
    names = ("frow", "fcol", "chan")
    place = {name: lax.axis_index(name) for name in names}
    count = {name: lax.axis_size(name) for name in names}
    me = place["chan"]
    partner = 1 - me
    mesh_ids = pl.DeviceIdType.MESH
    own = cube.at[me]

    halves = []
    for index, which in enumerate((partner, me)):
        at = pl.ds(pl.multiple_of(which * half, half), half)
        halves.append(pltpu.make_async_copy(
            image_ref.at[:, at], raw.at[:, at], local_sems.at[index]))
        halves[-1].start()
    keep_levels = pltpu.make_async_copy(weights_ref, level_rows, local_sems.at[2])
    keep_levels.start()

    def target(row_step, col_step):
        return (place["frow"] + row_step, place["fcol"] + col_step, me)

    def exists(row_step, col_step):
        found = None
        for name, step in (("frow", row_step), ("fcol", col_step)):
            if step:
                here = place[name] < count[name] - 1 if step > 0 else place[name] > 0
                found = here if found is None else found & here
        return found

    around = [(r, c) for r in (-1, 0, 1) for c in (-1, 0, 1) if (r, c) != (0, 0)]
    has = {key: exists(*key) for key in around}
    mate = (place["frow"], place["fcol"], partner)
    barrier = pltpu.get_barrier_semaphore()
    pl.semaphore_signal(barrier, inc=1, device_id=mate, device_id_type=mesh_ids)
    friends = 1
    for key in around:

        @pl.when(has[key])
        def _(key=key):
            pl.semaphore_signal(barrier, inc=1, device_id=target(*key), device_id_type=mesh_ids)

        friends = friends + jnp.where(has[key], 1, 0)

    def flatten_part(which):
        def body(step, carried):
            at = pl.multiple_of(which * half + step * 8, 8)
            own[pl.ds(HALO + at, 8)] = jnp.swapaxes(raw[:, pl.ds(at, 8), :], 0, 1)
            return carried

        lax.fori_loop(0, half // 8, body, 0)

    halves[0].wait()
    flatten_part(partner)
    pl.semaphore_wait(barrier, friends)

    used = [0]

    def copy_to(source, sink, device):
        index = used[0]
        used[0] += 1
        return pltpu.make_async_remote_copy(
            src_ref=source, dst_ref=sink, send_sem=send_sems.at[index],
            recv_sem=recv_sems.at[index], device_id=device, device_id_type=mesh_ids,
        )

    def cube_parts(owner, which):
        parts = []
        for chunk in range(chunks):
            at = pl.ds(HALO + which * half + chunk * CHUNK, CHUNK)
            parts.append(copy_to(cube.at[owner, at], cube.at[owner, at], mate))
        return parts

    first_parts = cube_parts(me, partner)
    for copy in first_parts:
        copy.start()

    def start_all(copies):
        for goes, _, copy in copies:

            @pl.when(has[goes])
            def _(copy=copy):
                copy.start()

    def arrive_all(copies):
        for _, comes, copy in copies:

            @pl.when(has[comes])
            def _(copy=copy):
                copy.wait_recv()

    def left_all(copies):
        for goes, _, copy in copies:

            @pl.when(has[goes])
            def _(copy=copy):
                copy.wait_send()

    def row_copies(ref, reach):
        top = lambda at: ref.at[pl.ds(at, reach)]
        return [
            ((1, 0), (-1, 0), copy_to(top(HALO + rows - reach), top(HALO - reach), target(1, 0))),
            ((-1, 0), (1, 0), copy_to(top(HALO), top(HALO + rows), target(-1, 0))),
        ]

    def col_copies(out, strips, corners):
        copies = []
        for side, step in ((1, 1), (0, -1)):
            copies.append((
                (0, step), (0, -step),
                copy_to(out.at[side], strips.at[1 - side], target(0, step)),
            ))
            for low, turn in ((0, 1), (1, -1)):
                group = groups - 1 if turn == 1 else 0
                copies.append((
                    (turn, step), (-turn, -step),
                    copy_to(out.at[side, :, group], corners.at[1 - side, low], target(turn, step)),
                ))
        return copies

    lane = lax.broadcasted_iota(jnp.int32, (channels, wide), 1)
    early = lane < 64

    def pack_edges(ref, out, kind):
        def body(group, carried):
            left = right = jnp.zeros((channels, wide), jnp.float32)
            for slot in range(PACK):
                at = HALO + group * PACK + slot
                here = (lane >= slot * 8) & (lane < slot * 8 + 8)
                edge = pltpu.roll(ref[at, :, :wide], slot * 8, 1)
                left = jnp.where(here, edge, left)
                edge = pltpu.roll(ref[at, :, cols - wide :], (slot * 8 + 8) % wide, 1)
                right = jnp.where(here, edge, right)
            out[0, kind, group] = left
            out[1, kind, group] = right
            return carried

        lax.fori_loop(0, groups, body, 0)

    def clear_edges(strips, corners):
        for side, step in ((0, -1), (1, 1)):

            @pl.when(jnp.logical_not(has[(0, step)]))
            def _(side=side):
                strips[side] = jnp.zeros(strips.shape[1:], jnp.float32)

            for low, turn in ((0, -1), (1, 1)):

                @pl.when(jnp.logical_not(has[(turn, step)]))
                def _(side=side, low=low):
                    corners[side, low] = jnp.zeros(corners.shape[2:], jnp.float32)

    def clear_rows(ref, first, last, reach):
        zero = jnp.zeros((reach, channels, cols), jnp.float32)

        @pl.when(jnp.logical_not(has[(-1, 0)]))
        def _():
            ref[pl.ds(first, reach)] = zero

        @pl.when(jnp.logical_not(has[(1, 0)]))
        def _():
            ref[pl.ds(last, reach)] = zero

    halves[1].wait()
    flatten_part(me)
    rows_one = row_copies(own, REACH)
    start_all(rows_one)
    pack_edges(own, strips_out, 0)
    cols_one = col_copies(strips_out, strips_in, corners_in)
    start_all(cols_one)
    clear_rows(own, HALO - REACH, HALO + rows, REACH)
    clear_edges(strips_in, corners_in)
    clear_edges(strips_in_two, corners_in_two)
    for kind, reach in ((0, NEAR), (1, REACH)):
        clear_rows(diffs.at[kind], HALO - reach, HALO + rows, reach)
    gram[...] = jnp.zeros(gram.shape, jnp.float32)

    for side in range(2):
        plain, forward, backward = column_weights(
            place["fcol"] * cols + side * wide, count["fcol"] * cols
        )
        plain, forward, backward = [
            jnp.concatenate([values, values], axis=0).astype(jnp.bfloat16)
            for values in (plain, forward, backward)
        ]
        taps_one[side, :, :wide] = plain
        taps_one[side, :, wide:] = forward
        taps_two[side] = backward

    def doubled(ref, strips, corners, kind, group):
        if group is None:
            line = lambda slot: slot if slot < HALO else slot + rows
            edge = lambda side, slot: (corners[side, 0 if slot < HALO else 1, kind],
                                       (slot + HALO) % PACK)
        else:
            line = lambda slot: HALO + group * PACK + slot
            edge = lambda side, slot: (strips[side, kind, group], slot)
        lefts, rights = [], []
        for slot in range(PACK):
            first, second = ref[line(slot), :, :wide], ref[line(slot), :, wide:]
            before, at = edge(0, slot)
            before = pltpu.roll(before, (wide - 8 - at * 8) % wide, 1)
            after, at = edge(1, slot)
            after = pltpu.roll(after, (wide - at * 8) % wide, 1)
            lefts.append(jnp.concatenate([first, jnp.where(early, second, before)], axis=1))
            rights.append(jnp.concatenate([second, jnp.where(early, after, first)], axis=1))
        return [
            jnp.concatenate(split_two(jnp.concatenate(pieces, axis=0)), axis=1)
            for pieces in (lefts, rights)
        ]

    def store_lines(ref, group, lanes_at, values):
        values = values.reshape(PACK, channels, wide)
        if group is None:
            ref[pl.ds(0, HALO), :, lanes_at] = values[:HALO]
            ref[pl.ds(HALO + rows, HALO), :, lanes_at] = values[HALO:]
        else:
            ref[pl.ds(HALO + group * PACK, PACK), :, lanes_at] = values

    dot = functools.partial(jnp.dot, preferred_element_type=jnp.float32)
    spots = (slice(0, wide), slice(wide, cols))

    def analyse(group):
        for side, values in enumerate(doubled(own, strips_in, corners_in, 0, group)):
            both = dot(values, taps_one[side])
            store_lines(one_cols, group, spots[side], both[:, :wide])
            store_lines(two_cols, group, spots[side], both[:, wide:])

    def each_group(work):
        def body(group, carried):
            work(group)
            return carried

        lax.fori_loop(0, groups, body, 0)
        work(None)

    arrive_all(rows_one)
    arrive_all(cols_one)
    each_group(analyse)

    def smooth_rows(step, carried):
        at = HALO - 4 + step * 8
        middle[pl.ds(at, 8)] = rows_filter(two_cols, at, 8, 1)
        return carried

    lax.fori_loop(0, (rows + 8) // 8, smooth_rows, 0)
    clear_rows(middle, HALO - 4, HALO + rows, 4)

    def collect(step, carried):
        at = pl.multiple_of(step * 8, 8)
        first = rows_filter(one_cols, HALO + at, 8, 1)
        second = rows_filter(middle, HALO + at, 8, 2)
        coarse[0, pl.ds(at, 8)] = first
        coarse[1, pl.ds(at, 8)] = second
        bands = (own[pl.ds(HALO + at, 8)] - first, first - second, second)
        for index, band in enumerate(bands):
            square = band * band
            folded = square[:, :8]
            for start in range(8, channels, 8):
                folded = folded + square[:, start : start + 8]
            sums[index, pl.ds(at, 8)] = jnp.sum(jnp.swapaxes(folded, 0, 1), axis=0)
        return carried

    lax.fori_loop(0, rows // 8, collect, 0)
    share_sums = [copy_to(sums.at[index], other_sums.at[index], mate) for index in range(3)]
    share_sums[0].start()

    block = 4

    def gram_step(step, total):
        at = HALO + me * half + step * block
        sides = [
            jnp.concatenate([cube[side, at + row] for row in range(block)], axis=1)
            for side in range(2)
        ]
        both = jnp.concatenate(split_two(jnp.concatenate(sides, axis=0)), axis=0)
        return total + lax.dot_general(
            both, both, (((1,), (1,)), ((), ())), preferred_element_type=jnp.float32
        )

    product = jnp.zeros((2 * order, 2 * order), jnp.float32)
    for chunk, copy in enumerate(first_parts):
        copy.wait_recv()
        product = lax.fori_loop(
            chunk * CHUNK // block, (chunk + 1) * CHUNK // block, gram_step, product
        )
    gram[:, :order] = (
        product[:order, :order] + (product[:order, order:] + product[order:, :order])
    ) + product[order:, order:]
    share_gram = copy_to(gram, other_gram, mate)
    share_gram.start()
    share_sums[1].start()
    share_sums[2].start()
    second_parts = cube_parts(me, me)
    for copy in second_parts:
        copy.start()

    row = lax.broadcasted_iota(jnp.int32, (8, gram.shape[1]), 0)
    spot = lax.broadcasted_iota(jnp.int32, (channels, gram.shape[1]), 0)
    marks = (row, spot == 1, spot == channels - 1)

    def turns(step, carry):
        for index in range(TURNS):
            at = lax.rem(step * TURNS + index + 1, order - 1)
            carry = rank_round(carry, first_on_top(at, spot.shape), marks)
        return carry

    share_gram.wait_recv()
    state = rank_start(gram[...] + other_gram[...], marks)
    steps = JSWEEPS * (order - 1) // TURNS
    pause = steps // 6
    state = lax.fori_loop(0, pause, turns, state)
    keep_levels.wait()
    for index in range(3):
        share_sums[index].wait_recv()
        levels = band_levels[index] * level_rows[index]
        totals = sums[index] + other_sums[index]
        factors[index] = levels / jnp.sqrt(jnp.maximum(totals, levels * levels))

    def project(step, carried):
        base = pl.multiple_of(step * 8, 8)
        scales = [factors[index, pl.ds(base, 8)] for index in range(3)]
        for line in range(8):
            at = base + line
            first, second = coarse[0, at], coarse[1, at]
            bands = (own[HALO + at] - first, first - second, second)
            dual = [
                band * jnp.broadcast_to(scale[line : line + 1], band.shape)
                for band, scale in zip(bands, scales)
            ]
            duals[at] = dual[0]
            diffs[0, HALO + at] = dual[1] - dual[0]
            diffs[1, HALO + at] = dual[2] - dual[1]
        return carried

    lax.fori_loop(0, rows // 8, project, 0)
    rows_two = row_copies(diffs.at[1], REACH) + row_copies(diffs.at[0], NEAR)
    start_all(rows_two)
    for kind in range(2):
        pack_edges(diffs.at[kind], strips_out_two, kind)
    cols_two = col_copies(strips_out_two, strips_in_two, corners_in_two)
    start_all(cols_two)
    state = lax.fori_loop(pause, steps, turns, state)
    mixing[...] = rank_finish(state, threshold)

    arrive_all(rows_two)
    arrive_all(cols_two)

    def synthesise(group):
        edges = (strips_in_two, corners_in_two)
        for side, values in enumerate(doubled(diffs.at[0], *edges, 0, group)):
            store_lines(one_cols, group, spots[side], dot(values, taps_one[side, :, :wide]))
        for side, values in enumerate(doubled(diffs.at[1], *edges, 1, group)):
            store_lines(two_cols, group, spots[side], dot(values, taps_two[side]))

    each_group(synthesise)

    def gather_rows(step, carried):
        at = HALO - NEAR + step * 4
        middle[pl.ds(at, 4)] = one_cols[pl.ds(at, 4)] + rows_filter(two_cols, at, 4, 2)
        return carried

    lax.fori_loop(0, (rows + 2 * NEAR) // 4, gather_rows, 0)
    clear_rows(middle, HALO - NEAR, HALO + rows, NEAR)

    def deliver(step, carried):
        at = pl.multiple_of(step * 8, 8)
        result = duals[pl.ds(at, 8)] + rows_filter(middle, HALO + at, 8, 1)
        back_ref[:, pl.ds(at, 8), :] = jnp.swapaxes(result, 0, 1)
        return carried

    lax.fori_loop(0, rows // 8, deliver, 0)

    own_rows = pl.ds(pl.multiple_of(me * channels, channels), channels)
    high, low = split_two(mixing[own_rows, :order])
    left = jnp.concatenate([high, high, low, low], axis=1)

    def rank_block(at):
        lines = []
        for line in range(8):
            values = jnp.concatenate(
                [cube[0, HALO + at + line], cube[1, HALO + at + line]], axis=0
            )
            high, low = split_two(values)
            lines.append(dot(left, jnp.concatenate([high, low, high, low], axis=0)))
        result = jnp.concatenate([values[None] for values in lines], axis=0)
        rank_ref[:, pl.ds(at, 8), :] = jnp.swapaxes(result, 0, 1)

    def rank_step(step, carried):
        rank_block(pl.multiple_of(me * half + step * 8, 8))
        return carried

    lax.fori_loop(0, half // 8, rank_step, 0)
    for chunk, copy in enumerate(second_parts):
        copy.wait_recv()
        for step in range(CHUNK // 8):
            rank_block(pl.multiple_of(partner * half + chunk * CHUNK + step * 8, 8))
    for copies in (rows_one, cols_one, rows_two, cols_two):
        left_all(copies)
    for copy in (*first_parts, *second_parts, *share_sums, share_gram):
        copy.wait_send()


def shards(image_cube, weights):
    channels, rows, cols = image_cube.shape
    threshold = rank_level * math.sqrt(rows * cols)
    order = channels * lax.axis_size("chan")
    tall = rows + 2 * HALO
    groups = rows // PACK
    f32 = jnp.float32
    in_hbm = pl.BlockSpec(memory_space=pltpu.HBM)
    in_vmem = pl.BlockSpec(memory_space=pltpu.VMEM)
    vmem = pltpu.VMEM
    lines = (tall, channels, cols)
    copies = 64
    return pl.pallas_call(
        functools.partial(facet_kernel, threshold),
        out_shape=(
            jax.ShapeDtypeStruct(image_cube.shape, f32),
            jax.ShapeDtypeStruct(image_cube.shape, f32),
        ),
        in_specs=[in_hbm, in_hbm],
        out_specs=(in_vmem, in_vmem),
        scratch_shapes=[
            vmem(image_cube.shape, f32),
            vmem((3, rows, cols), f32),
            vmem((2, *lines), f32),
            vmem(lines, f32),
            vmem(lines, f32),
            vmem(lines, f32),
            vmem((2, rows, channels, cols), f32),
            vmem((3, rows, cols), f32),
            vmem((3, rows, cols), f32),
            vmem((3, rows, cols), f32),
            vmem((rows, channels, cols), f32),
            vmem((2, *lines), f32),
            vmem((order, 128), f32),
            vmem((order, 128), f32),
            vmem((128, 128), f32),
            vmem((2, 512, 256), jnp.bfloat16),
            vmem((2, 512, 128), jnp.bfloat16),
            vmem((2, 1, groups, channels, 128), f32),
            vmem((2, 1, groups, channels, 128), f32),
            vmem((2, 2, 1, channels, 128), f32),
            vmem((2, 2, groups, channels, 128), f32),
            vmem((2, 2, groups, channels, 128), f32),
            vmem((2, 2, 2, channels, 128), f32),
            pltpu.SemaphoreType.DMA((copies,)),
            pltpu.SemaphoreType.DMA((copies,)),
            pltpu.SemaphoreType.DMA((3,)),
        ],
        compiler_params=pltpu.CompilerParams(
            collective_id=0, has_side_effects=True, vmem_limit_bytes=50 * 2**20
        ),
    )(image_cube, weights)


def solution(mesh):
    placed = (P("chan", "frow", "fcol"), P(None, "frow", "fcol"))
    return jax.shard_map(
        shards,
        mesh=mesh,
        in_specs=placed,
        out_specs=(P("chan", "frow", "fcol"), P("chan", "frow", "fcol")),
        check_vma=False,
    )
```

time: 57.5 us -> 41.7 us (0.73)
  Pallas kernels: 52.3 us -> 36.6 us
    pallas_call x1, Pallas kernels: 52.3 us -> 36.6 us  [shards(): pl.pallas_call(functools.partial(facet_kernel, threshold), out_shape=(jax...]
where the time goes in v1:
time: 41.7 us; the launch traced here: 41.4 us
  Pallas kernels  36.6 us (88%)
  local copies, waits for them, and re-layouts  4.09 us (10%)
  between operations  0.65 us (2%)
    pallas_call x1, Pallas kernels, shards(): pl.pallas_call(functools.partial(facet_kernel, threshold), out_shape=(jax...  36.6 us
    unnamed x6, local copies, waits for them, and re-layouts  4.09 us

profile of v1, /device:TPU:1, one launch (start us, length us, event | category | flops | bytes accessed | tf_op | source)
XLA Modules:
  0.0 41.4 jit_solution(3825216480906373282)
XLA Ops:
  0.6 0.0 copy-start
  0.6 1.2 %copy-done = f32[16,64,256]{2,1,0:T(8,128)S(1)} copy-done((f32[16,64,256]{2,1,0:T(8,128)S(1)}, f32[16,64,256]{2,1,0:T(8,128)}, u32[]{:S(2)}) %copy-start) | copy-done | bytes 1048600
  1.9 0.0 copy-start.1
  1.9 0.9 %copy-done.1 = f32[3,64,256]{2,1,0:T(8,128)S(1)} copy-done((f32[3,64,256]{2,1,0:T(8,128)S(1)}, f32[3,64,256]{2,1,0:T(8,128)}, u32[]{:S(2)}) %copy-start.1) | copy-done | bytes 196632
  2.8 36.6 %shard_map.41 = (f32[16,64,256]{2,1,0:T(8,128)S(1)}, f32[16,64,256]{2,1,0:T(8,128)S(1)}) custom-call(f32[16,64,256]{2,1,0:T(8,128)S(1)} %copy-done, f32[3,64,256]{2,1,0:T(8,128)S(1)} %copy-done.1), custom_call_target="tpu_custom_call" | custom-call | tf_op jit(solution)/shard_map/pallas_call | solution.py:582
  39.4 1.0 %copy.6 = f32[16,64,256]{2,1,0:T(8,128)} copy(f32[16,64,256]{2,1,0:T(8,128)S(1)} %get-tuple-element.4) | data formatting | bytes 2097152
  40.4 1.0 %copy.7 = f32[16,64,256]{2,1,0:T(8,128)} copy(f32[16,64,256]{2,1,0:T(8,128)S(1)} %get-tuple-element.5) | data formatting | bytes 2097152
Async XLA Ops:
  0.6 1.2 %copy-start = (f32[16,64,256]{2,1,0:T(8,128)S(1)}, f32[16,64,256]{2,1,0:T(8,128)}, u32[]{:S(2)}) copy-start(f32[16,64,256]{2,1,0:T(8,128)} %image_ref.1) | copy-start | bytes 3145732
  1.9 0.9 %copy-start.1 = (f32[3,64,256]{2,1,0:T(8,128)S(1)}, f32[3,64,256]{2,1,0:T(8,128)}, u32[]{:S(2)}) copy-start(f32[3,64,256]{2,1,0:T(8,128)} %weights_ref.1) | copy-start | bytes 589828

commit v2 on v1

--- a/solution.py
+++ b/solution.py
@@ -579,6 +579,7 @@
     vmem = pltpu.VMEM
     lines = (tall, channels, cols)
     copies = 64
+    stay = lambda array: pltpu.with_memory_space_constraint(array, pltpu.HBM)
     return pl.pallas_call(
         functools.partial(facet_kernel, threshold),
         out_shape=(
@@ -618,7 +619,7 @@
         compiler_params=pltpu.CompilerParams(
             collective_id=0, has_side_effects=True, vmem_limit_bytes=50 * 2**20
         ),
-    )(image_cube, weights)
+    )(stay(image_cube), stay(weights))
 
 
 def solution(mesh):

time: 41.7 us -> 39.2 us (0.940)
  local copies, waits for them, and re-layouts: 4.09 us -> 1.94 us
    unnamed x6 -> x2, local copies, waits for them, and re-layouts: 4.09 us -> 1.94 us
where the time goes in v2:
time: 39.2 us; the launch traced here: 38.9 us
  Pallas kernels  36.3 us (93%)
  local copies, waits for them, and re-layouts  1.94 us (5%)
  between operations  0.64 us (2%)
    pallas_call x1, Pallas kernels, shards(): pl.pallas_call(functools.partial(facet_kernel, threshold), out_shape=(jax...  36.3 us
    unnamed x2, local copies, waits for them, and re-layouts  1.94 us

profile of v2, /device:TPU:1, one launch (start us, length us, event | category | flops | bytes accessed | tf_op | source)
XLA Modules:
  0.0 38.9 jit_solution(4934786700037340875)
XLA Ops:
  0.6 36.3 %shard_map.41 = (f32[16,64,256]{2,1,0:T(8,128)S(1)}, f32[16,64,256]{2,1,0:T(8,128)S(1)}) custom-call(f32[16,64,256]{2,1,0:T(8,128)} %image_ref.1, f32[3,64,256]{2,1,0:T(8,128)} %weights_ref.1), custom_call_target="tpu_custom_call" | custom-call | tf_op jit(solution)/shard_map/pallas_call | solution.py:583
  37.0 1.0 %copy.6 = f32[16,64,256]{2,1,0:T(8,128)} copy(f32[16,64,256]{2,1,0:T(8,128)S(1)} %get-tuple-element.4) | data formatting | bytes 2097152
  37.9 1.0 %copy.7 = f32[16,64,256]{2,1,0:T(8,128)} copy(f32[16,64,256]{2,1,0:T(8,128)S(1)} %get-tuple-element.5) | data formatting | bytes 2097152

commit v3 on v2

--- a/solution.py
+++ b/solution.py
@@ -14,7 +14,8 @@
 NEAR = 2
 PACK = 16
 CHUNK = 8
-TURNS = 3
+TURNS = 16
+PIECES = 4
 
 filter_taps = (0.0625, 0.25, 0.375, 0.25, 0.0625)
 band_levels = (12.0, 4.0, 2.5)
@@ -174,13 +175,16 @@
     mesh_ids = pl.DeviceIdType.MESH
     own = cube.at[me]
 
-    halves = []
-    for index, which in enumerate((partner, me)):
-        at = pl.ds(pl.multiple_of(which * half, half), half)
-        halves.append(pltpu.make_async_copy(
-            image_ref.at[:, at], raw.at[:, at], local_sems.at[index]))
-        halves[-1].start()
-    keep_levels = pltpu.make_async_copy(weights_ref, level_rows, local_sems.at[2])
+    loads = []
+    for chunk in range(chunks + 1):
+        if chunk < chunks:
+            at = pl.ds(pl.multiple_of(partner * half + chunk * CHUNK, CHUNK), CHUNK)
+        else:
+            at = pl.ds(pl.multiple_of(me * half, half), half)
+        loads.append(pltpu.make_async_copy(
+            image_ref.at[:, at], raw.at[:, at], local_sems.at[chunk]))
+        loads[-1].start()
+    keep_levels = pltpu.make_async_copy(weights_ref, level_rows, local_sems.at[chunks + 1])
     keep_levels.start()
 
     def target(row_step, col_step):
@@ -208,17 +212,13 @@
 
         friends = friends + jnp.where(has[key], 1, 0)
 
-    def flatten_part(which):
+    def flatten_part(start, size):
         def body(step, carried):
-            at = pl.multiple_of(which * half + step * 8, 8)
+            at = pl.multiple_of(start + step * 8, 8)
             own[pl.ds(HALO + at, 8)] = jnp.swapaxes(raw[:, pl.ds(at, 8), :], 0, 1)
             return carried
 
-        lax.fori_loop(0, half // 8, body, 0)
-
-    halves[0].wait()
-    flatten_part(partner)
-    pl.semaphore_wait(barrier, friends)
+        lax.fori_loop(0, size // 8, body, 0)
 
     used = [0]
 
@@ -238,7 +238,11 @@
         return parts
 
     first_parts = cube_parts(me, partner)
-    for copy in first_parts:
+    for chunk, copy in enumerate(first_parts):
+        loads[chunk].wait()
+        flatten_part(partner * half + chunk * CHUNK, CHUNK)
+        if chunk == 0:
+            pl.semaphore_wait(barrier, friends)
         copy.start()
 
     def start_all(copies):
@@ -327,8 +331,8 @@
         def _():
             ref[pl.ds(last, reach)] = zero
 
-    halves[1].wait()
-    flatten_part(me)
+    loads[chunks].wait()
+    flatten_part(me * half, half)
     rows_one = row_copies(own, REACH)
     start_all(rows_one)
     pack_edges(own, strips_out, 0)
@@ -430,6 +434,7 @@
     lax.fori_loop(0, rows // 8, collect, 0)
     share_sums = [copy_to(sums.at[index], other_sums.at[index], mate) for index in range(3)]
     share_sums[0].start()
+    share_sums[1].start()
 
     block = 4
 
@@ -455,7 +460,6 @@
     ) + product[order:, order:]
     share_gram = copy_to(gram, other_gram, mate)
     share_gram.start()
-    share_sums[1].start()
     share_sums[2].start()
     second_parts = cube_parts(me, me)
     for copy in second_parts:
@@ -465,17 +469,22 @@
     spot = lax.broadcasted_iota(jnp.int32, (channels, gram.shape[1]), 0)
     marks = (row, spot == 1, spot == channels - 1)
 
-    def turns(step, carry):
-        for index in range(TURNS):
-            at = lax.rem(step * TURNS + index + 1, order - 1)
-            carry = rank_round(carry, first_on_top(at, spot.shape), marks)
-        return carry
+    def turns(begin, end, carry):
+        size = max(step for step in range(1, TURNS + 1) if (end - begin) % step == 0)
+
+        def body(step, carry):
+            for index in range(size):
+                at = lax.rem(begin + step * size + index + 1, order - 1)
+                carry = rank_round(carry, first_on_top(at, spot.shape), marks)
+            return carry
+
+        return lax.fori_loop(0, (end - begin) // size, body, carry)
 
     share_gram.wait_recv()
     state = rank_start(gram[...] + other_gram[...], marks)
-    steps = JSWEEPS * (order - 1) // TURNS
-    pause = steps // 6
-    state = lax.fori_loop(0, pause, turns, state)
+    rounds = JSWEEPS * (order - 1)
+    pause = rounds // 6
+    state = turns(0, pause, state)
     keep_levels.wait()
     for index in range(3):
         share_sums[index].wait_recv()
@@ -506,7 +515,7 @@
         pack_edges(diffs.at[kind], strips_out_two, kind)
     cols_two = col_copies(strips_out_two, strips_in_two, corners_in_two)
     start_all(cols_two)
-    state = lax.fori_loop(pause, steps, turns, state)
+    state = turns(pause, rounds, state)
     mixing[...] = rank_finish(state, threshold)
 
     arrive_all(rows_two)
@@ -565,6 +574,19 @@
         left_all(copies)
     for copy in (*first_parts, *second_parts, *share_sums, share_gram):
         copy.wait_send()
+
+
+def output_kernel(back_ref, rank_ref, back_out, rank_out, sems):
+    copies = []
+    size = back_ref.shape[0] // PIECES
+    for source, sink in ((back_ref, back_out), (rank_ref, rank_out)):
+        for piece in range(PIECES):
+            at = pl.ds(piece * size, size)
+            copies.append(pltpu.make_async_copy(
+                source.at[at], sink.at[at], sems.at[len(copies)]))
+            copies[-1].start()
+    for copy in copies:
+        copy.wait()
 
 
 def shards(image_cube, weights):
@@ -580,7 +602,7 @@
     lines = (tall, channels, cols)
     copies = 64
     stay = lambda array: pltpu.with_memory_space_constraint(array, pltpu.HBM)
-    return pl.pallas_call(
+    held = pl.pallas_call(
         functools.partial(facet_kernel, threshold),
         out_shape=(
             jax.ShapeDtypeStruct(image_cube.shape, f32),
@@ -614,12 +636,23 @@
             vmem((2, 2, 2, channels, 128), f32),
             pltpu.SemaphoreType.DMA((copies,)),
             pltpu.SemaphoreType.DMA((copies,)),
-            pltpu.SemaphoreType.DMA((3,)),
+            pltpu.SemaphoreType.DMA((rows // 2 // CHUNK + 2,)),
         ],
         compiler_params=pltpu.CompilerParams(
             collective_id=0, has_side_effects=True, vmem_limit_bytes=50 * 2**20
         ),
     )(stay(image_cube), stay(weights))
+    return pl.pallas_call(
+        output_kernel,
+        out_shape=(
+            jax.ShapeDtypeStruct(image_cube.shape, f32),
+            jax.ShapeDtypeStruct(image_cube.shape, f32),
+        ),
+        in_specs=[in_vmem, in_vmem],
+        out_specs=(in_hbm, in_hbm),
+        scratch_shapes=[pltpu.SemaphoreType.DMA((2 * PIECES,))],
+        compiler_params=pltpu.CompilerParams(vmem_limit_bytes=4 * 2**20),
+    )(*held)
 
 
 def solution(mesh):

time: 39.2 us -> 37.1 us (0.946)
  local copies, waits for them, and re-layouts: 1.94 us -> 0 us
    unnamed x2 -> x0, local copies, waits for them, and re-layouts: 1.94 us -> none
    pallas_call x0 -> x1, Pallas kernels: none -> 1.38 us  [shards(): pl.pallas_call(output_kernel, out_shape=(jax.ShapeDtypeStruct(image_cube....]
    pallas_call x1, Pallas kernels: 36.3 us -> 35 us  [shards(): pl.pallas_call(functools.partial(facet_kernel, threshold), out_shape=(jax...]
where the time goes in v3:
time: 37.1 us; the launch traced here: 37 us
  Pallas kernels  36.3 us (98%)
  between operations  0.64 us (2%)
    pallas_call x1, Pallas kernels, shards(): pl.pallas_call(functools.partial(facet_kernel, threshold), out_shape=(jax...  35 us
    pallas_call x1, Pallas kernels, shards(): pl.pallas_call(output_kernel, out_shape=(jax.ShapeDtypeStruct(image_cube....  1.38 us

profile of v3, /device:TPU:1, one launch (start us, length us, event | category | flops | bytes accessed | tf_op | source)
XLA Modules:
  0.0 37.0 jit_solution(14923473540460475541)
XLA Ops:
  0.6 35.0 %shard_map.41 = (f32[16,64,256]{2,1,0:T(8,128)S(1)}, f32[16,64,256]{2,1,0:T(8,128)S(1)}) custom-call(f32[16,64,256]{2,1,0:T(8,128)} %image_ref.1, f32[3,64,256]{2,1,0:T(8,128)} %weights_ref.1), custom_call_target="tpu_custom_call" | custom-call | tf_op jit(solution)/shard_map/pallas_call | solution.py:605
  35.6 1.4 %shard_map.42 = (f32[16,64,256]{2,1,0:T(8,128)}, f32[16,64,256]{2,1,0:T(8,128)}) custom-call(f32[16,64,256]{2,1,0:T(8,128)S(1)} %get-tuple-element.4.back_ref, f32[16,64,256]{2,1,0:T(8,128)S(1)} %get-tuple-element.5.rank_ref), custom_call_target="tpu_custom_call" | custom-call | tf_op jit(solution)/shard_map/pallas_call | solution.py:645

commit v4 on v3

--- a/solution.py
+++ b/solution.py
@@ -14,7 +14,7 @@
 NEAR = 2
 PACK = 16
 CHUNK = 8
-TURNS = 16
+TURNS = 31
 PIECES = 4
 
 filter_taps = (0.0625, 0.25, 0.375, 0.25, 0.0625)
@@ -89,12 +89,10 @@
     shape = (half, gram.shape[1])
     place = lax.broadcasted_iota(jnp.int32, shape, 0)
     lane = lax.broadcasted_iota(jnp.int32, shape, 1)
-    flip_row = lax.broadcasted_iota(jnp.int32, (half, half), 0)
-    flip_lane = lax.broadcasted_iota(jnp.int32, (half, half), 1)
-    flip = jnp.where(flip_row + flip_lane == half - 1, 1.0, 0.0)
-    low = jnp.dot(
-        flip, gram[half:], precision=lax.Precision.HIGHEST, preferred_element_type=jnp.float32
-    )
+    low = jnp.zeros(shape, jnp.float32)
+    for index in range(half):
+        line = gram[2 * half - 1 - index : 2 * half - index]
+        low = jnp.where(place == index, jnp.broadcast_to(line, shape), low)
     sides = (jnp.where(lane == place, 1.0, 0.0), jnp.where(lane == 2 * half - 1 - place, 1.0, 0.0))
     vectors = (gram[:half], low, *sides)
     diag = (lanes(gram[:half] * sides[0]), lanes(low * sides[1]))
@@ -104,14 +102,12 @@
 
 def rank_finish(carry, threshold):
     vectors, diag = carry[0], carry[1]
-    mixing = 0.0
-    for side, values in zip(vectors[2:], diag):
-        factor = 1.0 - threshold / jnp.sqrt(jnp.maximum(values, threshold * threshold))
-        mixing = mixing + lax.dot_general(
-            side * factor, side, (((0,), (0,)), ((), ())),
-            precision=lax.Precision.HIGHEST, preferred_element_type=jnp.float32,
-        )
-    return mixing
+    sides, values = jnp.concatenate(vectors[2:], axis=0), jnp.concatenate(diag, axis=0)
+    factor = 1.0 - threshold / jnp.sqrt(jnp.maximum(values, threshold * threshold))
+    return lax.dot_general(
+        sides * factor, sides, (((0,), (0,)), ((), ())),
+        precision=lax.Precision.HIGHEST, preferred_element_type=jnp.float32,
+    )
 
 
 def split_two(values):
@@ -175,6 +171,31 @@
     mesh_ids = pl.DeviceIdType.MESH
     own = cube.at[me]
 
+    def target(row_step, col_step):
+        return (place["frow"] + row_step, place["fcol"] + col_step, me)
+
+    def exists(row_step, col_step):
+        found = None
+        for name, step in (("frow", row_step), ("fcol", col_step)):
+            if step:
+                here = place[name] < count[name] - 1 if step > 0 else place[name] > 0
+                found = here if found is None else found & here
+        return found
+
+    around = [(r, c) for r in (-1, 0, 1) for c in (-1, 0, 1) if (r, c) != (0, 0)]
+    has = {key: exists(*key) for key in around}
+    mate = (place["frow"], place["fcol"], partner)
+    barrier = pltpu.get_barrier_semaphore()
+    pl.semaphore_signal(barrier, inc=1, device_id=mate, device_id_type=mesh_ids)
+    friends = 1
+    for key in around:
+
+        @pl.when(has[key])
+        def _(key=key):
+            pl.semaphore_signal(barrier, inc=1, device_id=target(*key), device_id_type=mesh_ids)
+
+        friends = friends + jnp.where(has[key], 1, 0)
+
     loads = []
     for chunk in range(chunks + 1):
         if chunk < chunks:
@@ -186,31 +207,6 @@
         loads[-1].start()
     keep_levels = pltpu.make_async_copy(weights_ref, level_rows, local_sems.at[chunks + 1])
     keep_levels.start()
-
-    def target(row_step, col_step):
-        return (place["frow"] + row_step, place["fcol"] + col_step, me)
-
-    def exists(row_step, col_step):
-        found = None
-        for name, step in (("frow", row_step), ("fcol", col_step)):
-            if step:
-                here = place[name] < count[name] - 1 if step > 0 else place[name] > 0
-                found = here if found is None else found & here
-        return found
-
-    around = [(r, c) for r in (-1, 0, 1) for c in (-1, 0, 1) if (r, c) != (0, 0)]
-    has = {key: exists(*key) for key in around}
-    mate = (place["frow"], place["fcol"], partner)
-    barrier = pltpu.get_barrier_semaphore()
-    pl.semaphore_signal(barrier, inc=1, device_id=mate, device_id_type=mesh_ids)
-    friends = 1
-    for key in around:
-
-        @pl.when(has[key])
-        def _(key=key):
-            pl.semaphore_signal(barrier, inc=1, device_id=target(*key), device_id_type=mesh_ids)
-
-        friends = friends + jnp.where(has[key], 1, 0)
 
     def flatten_part(start, size):
         def body(step, carried):
@@ -355,7 +351,8 @@
         ]
         taps_one[side, :, :wide] = plain
         taps_one[side, :, wide:] = forward
-        taps_two[side] = backward
+        taps_two[side, :, :wide] = plain
+        taps_two[side, :, wide:] = backward
 
     def doubled(ref, strips, corners, kind, group):
         if group is None:
@@ -523,10 +520,12 @@
 
     def synthesise(group):
         edges = (strips_in_two, corners_in_two)
-        for side, values in enumerate(doubled(diffs.at[0], *edges, 0, group)):
-            store_lines(one_cols, group, spots[side], dot(values, taps_one[side, :, :wide]))
-        for side, values in enumerate(doubled(diffs.at[1], *edges, 1, group)):
-            store_lines(two_cols, group, spots[side], dot(values, taps_two[side]))
+        kinds = [doubled(diffs.at[kind], *edges, kind, group) for kind in range(2)]
+        for side, values in enumerate(zip(*kinds)):
+            both = dot(jnp.concatenate(values, axis=0), taps_two[side])
+            outer, inner = both[: PACK * channels], both[PACK * channels :]
+            store_lines(one_cols, group, spots[side], outer[:, :wide])
+            store_lines(two_cols, group, spots[side], inner[:, wide:])
 
     each_group(synthesise)
 
@@ -627,7 +626,7 @@
             vmem((order, 128), f32),
             vmem((128, 128), f32),
             vmem((2, 512, 256), jnp.bfloat16),
-            vmem((2, 512, 128), jnp.bfloat16),
+            vmem((2, 512, 256), jnp.bfloat16),
             vmem((2, 1, groups, channels, 128), f32),
             vmem((2, 1, groups, channels, 128), f32),
             vmem((2, 2, 1, channels, 128), f32),

time: 37.1 us -> 36.8 us (level)
  no operation moved by 1% of the time
where the time goes in v4:
time: 36.8 us; the launch traced here: 36.7 us
  Pallas kernels  36 us (98%)
  between operations  0.64 us (2%)
    pallas_call x1, Pallas kernels, shards(): pl.pallas_call(functools.partial(facet_kernel, threshold), out_shape=(jax...  34.6 us
    pallas_call x1, Pallas kernels, shards(): pl.pallas_call(output_kernel, out_shape=(jax.ShapeDtypeStruct(image_cube....  1.38 us

profile of v4, /device:TPU:1, one launch (start us, length us, event | category | flops | bytes accessed | tf_op | source)
XLA Modules:
  0.0 36.7 jit_solution(14535697774835827465)
XLA Ops:
  0.6 34.6 %shard_map.41 = (f32[16,64,256]{2,1,0:T(8,128)S(1)}, f32[16,64,256]{2,1,0:T(8,128)S(1)}) custom-call(f32[16,64,256]{2,1,0:T(8,128)} %image_ref.1, f32[3,64,256]{2,1,0:T(8,128)} %weights_ref.1), custom_call_target="tpu_custom_call" | custom-call | tf_op jit(solution)/shard_map/pallas_call | solution.py:604
  35.3 1.4 %shard_map.42 = (f32[16,64,256]{2,1,0:T(8,128)}, f32[16,64,256]{2,1,0:T(8,128)}) custom-call(f32[16,64,256]{2,1,0:T(8,128)S(1)} %get-tuple-element.4.back_ref, f32[16,64,256]{2,1,0:T(8,128)S(1)} %get-tuple-element.5.rank_ref), custom_call_target="tpu_custom_call" | custom-call | tf_op jit(solution)/shard_map/pallas_call | solution.py:644
